TPU v7x, 32 devices: a whole 2x2x4 slice. The times are simulated.
32 devices in a mesh: seq: 2 (over x), fsdp: 16 (over z, y, core).
Axes of the slice: x: 2, y: 2, z: 4, core: 2. Of those that a mesh axis runs over, the one named last changes fastest.
Arguments:
- incoming_state: bfloat16 [16, 512, 768], P('fsdp', 'seq'), may hold values from -6 to 6
- projection_matrix_triple: bfloat16 [768, 2304], P(('seq', 'fsdp')), may hold values from -0.3125 to 0.3125
- merge_matrix: bfloat16 [768, 768], P(('seq', 'fsdp')), may hold values from -1.75 to 1.75
- widen_matrix: bfloat16 [768, 3072], P(('seq', 'fsdp')), may hold values from -0.21875 to 0.21875
- shrink_matrix: bfloat16 [3072, 768], P(('seq', 'fsdp')), may hold values from -0.109375 to 0.109375
- offset_table: bfloat16 [6, 768], P(None, ('seq', 'fsdp')), may hold values from -1.5 to 1.5
- norm_scales: bfloat16 [2, 768], P(None, ('seq', 'fsdp')), may hold values from 0.25 to 1.75
- widen_offset: bfloat16 [3072], P(('seq', 'fsdp')), may hold values from -1.5 to 1.5
- trainable_gate_scores: float32 [12, 512, 512], P('seq', 'fsdp'), may hold values from -8 to 8
- gate_perturbation: float32 [12, 512, 512], P('seq', 'fsdp'), may hold values from -6 to 6
- softening_scale: float32 [12], P('seq'), may hold values from 0.5 to 2
- passage_extents: int32 [32], replicated, may hold values from 1 to 512, 8192 in all
- result_cotangent: bfloat16 [16, 512, 768], P('fsdp', 'seq'), may hold values from -6 to 6
Outputs:
- layer_out: bfloat16 [16, 512, 768], P('fsdp', 'seq')
- input_grad: float32 [16, 512, 768], P('fsdp', 'seq')
- grad_w_qkv: float32 [768, 2304], P(('seq', 'fsdp'))
- grad_w_out: float32 [768, 768], P(('seq', 'fsdp'))
- grad_w_up: float32 [768, 3072], P(('seq', 'fsdp'))
- grad_w_down: float32 [3072, 768], P(('seq', 'fsdp'))
- grad_biases: float32 [6, 768], P(None, ('seq', 'fsdp'))
- grad_gains: float32 [2, 768], P(None, ('seq', 'fsdp'))
- grad_bias_up: float32 [3072], P(('seq', 'fsdp'))
- mask_logit_gradient: float32 [12, 512, 512], P('seq', 'fsdp')
Inputs may be any that keep to these rules, and one draw needn't show every extreme that they name: `passage_extents`: they sum to 8192, and the longest is exactly 512.
All inputs are finite; a program needn't handle non-finite values.
Results may differ from a plain program's by a relative error of at most 0.013.
Values may be sent and summed in bfloat16 or wider, within the bound.
No kernel may reach another device: no remote copies, remote signals or barrier semaphores. Data moves between devices by JAX's collectives and lax.ppermute only.
A program may use at most 192 MiB of HBM per device.

v0:
```python
from functools import partial

import jax
import jax.numpy as jnp
from jax import lax
from jax.sharding import PartitionSpec as P

D = 768
FOCUS_COUNT = 12
HDIM = 64
MPOS = 512


EPS = 1e-05


def padded(block, sides, width):
    for axis, dim in sides:
        count = lax.axis_size(axis)
        forward = [(i, i + 1) for i in range(count - 1)]
        backward = [(target, source) for source, target in forward]
        low = lax.ppermute(
            lax.slice_in_dim(block, block.shape[dim] - width, None, axis=dim), axis, forward
        )
        high = lax.ppermute(lax.slice_in_dim(block, 0, width, axis=dim), axis, backward)
        block = jnp.concatenate([low, block, high], axis=dim)
    return block


def as_sent(value):
    return jax.tree.map(lambda a: a.astype(jnp.bfloat16) if a.dtype == jnp.float32 else a, value)


def shifted(value, axis, steps):
    count = lax.axis_size(axis)
    leading, last = (max(0, -steps), min(count, count - steps))
    return lax.ppermute(value, axis, [(source, source + steps) for source in range(leading, last)])


def layer_norm(values, gain, shift):
    center = values - jnp.mean(values, axis=-1, keepdims=True)
    spread = jnp.mean(center * center, axis=-1, keepdims=True)
    return center * lax.rsqrt(spread + EPS) * gain + shift


def locate(index, passage_opening, passage_finish, stream_rows):
    document = jnp.sum((passage_finish[None, :] <= index[:, None]).astype(jnp.int32), axis=1)
    begin = jnp.max(
        jnp.where(passage_opening[None, :] <= index[:, None], passage_opening[None, :], 0), axis=1
    )
    inside = (index >= 0) & (index < stream_rows)
    document = jnp.where(inside, document, -1)
    position = (index - begin) % MPOS
    return (document, position)


def one_hot_rows(positions):
    return (positions[:, None] == jnp.arange(MPOS, dtype=jnp.int32)[None, :]).astype(jnp.bfloat16)


def plain_dot(left, right):
    return jnp.dot(left, right, preferred_element_type=jnp.float32)


def left_dot(left, right):
    return lax.dot_general(
        left, right, (((0,), (0,)), ((), ())), preferred_element_type=jnp.float32
    )


def right_dot(left, right):
    return lax.dot_general(
        left, right, (((1,), (1,)), ((), ())), preferred_element_type=jnp.float32
    )


def lookup_of(table, rows_hot, cols_hot):
    picked = plain_dot(rows_hot, table).astype(jnp.bfloat16)
    return right_dot(picked, cols_hot)


def token_forward(
    tokens,
    context_tok,
    merge_matrix,
    widen_matrix,
    shrink_matrix,
    offset_table,
    norm_scales,
    widen_offset,
):
    small = offset_table.astype(jnp.float32)
    gain_rows = norm_scales.astype(jnp.float32)
    attn = plain_dot(context_tok, merge_matrix) + small[2]
    hidden_one = tokens.astype(jnp.float32) + attn
    normed = layer_norm(hidden_one, gain_rows[0], small[4])
    normed_low = normed.astype(jnp.bfloat16)
    up = plain_dot(normed_low, widen_matrix) + widen_offset.astype(jnp.float32)
    act_low = jax.nn.gelu(up, approximate=False).astype(jnp.bfloat16)
    hidden_two = normed + (plain_dot(act_low, shrink_matrix) + small[3])
    return (hidden_one, normed, normed_low, up, act_low, hidden_two)


def per_device(
    incoming_state,
    projection_matrix_triple,
    merge_matrix,
    widen_matrix,
    shrink_matrix,
    offset_table,
    norm_scales,
    widen_offset,
    trainable_gate_scores,
    gate_perturbation,
    softening_scale,
    passage_extents,
    result_cotangent,
):
    tok_rows = incoming_state.shape[1]
    tokens = incoming_state.reshape(tok_rows, D)
    seq_count = lax.axis_size("seq")
    head_count = FOCUS_COUNT // seq_count
    head_width = head_count * HDIM
    group_rows = tok_rows * seq_count
    stream_rows = group_rows * lax.axis_size("fsdp")
    block_rows = min(512, group_rows)
    window_rows = 3 * group_rows
    offsets_turned = offset_table.T
    gains_turned = norm_scales.T
    params = (
        lax.all_gather(projection_matrix_triple, ("seq", "fsdp"), axis=0, tiled=True),
        lax.all_gather(merge_matrix, ("seq", "fsdp"), axis=0, tiled=True),
        lax.all_gather(widen_matrix, ("seq", "fsdp"), axis=0, tiled=True),
        lax.all_gather(shrink_matrix, ("seq", "fsdp"), axis=0, tiled=True),
        lax.all_gather(offsets_turned, ("seq", "fsdp"), axis=0, tiled=True),
        lax.all_gather(gains_turned, ("seq", "fsdp"), axis=0, tiled=True),
        lax.all_gather(widen_offset, ("seq", "fsdp"), axis=0, tiled=True),
    )
    full_qkv, full_out, full_up, full_down = (params[0], params[1], params[2], params[3])
    full_biases = params[4].T
    full_gains = params[5].T
    full_bias_up = params[6]
    small = full_biases.astype(jnp.float32)
    gain_rows = full_gains.astype(jnp.float32)
    relaxed_mask_rows = jax.nn.sigmoid(
        (trainable_gate_scores + gate_perturbation) / softening_scale[:, None, None]
    )
    smooth_gate = lax.all_gather(relaxed_mask_rows.astype(jnp.bfloat16), "fsdp", axis=1, tiled=True)
    passage_finish = jnp.cumsum(passage_extents)
    passage_opening = passage_finish - passage_extents
    first = lax.axis_index("fsdp") * group_rows
    query_doc, query_pos = locate(
        first + jnp.arange(group_rows, dtype=jnp.int32),
        passage_opening,
        passage_finish,
        stream_rows,
    )
    key_doc, key_pos = locate(
        first - group_rows + jnp.arange(window_rows, dtype=jnp.int32),
        passage_opening,
        passage_finish,
        stream_rows,
    )
    query_hot = one_hot_rows(query_pos)
    key_hot = one_hot_rows(key_pos)
    qkv_bias = jnp.concatenate([small[0], jnp.zeros((D,), jnp.float32), small[1]])
    qkv = (
        (plain_dot(tokens, full_qkv) + qkv_bias)
        .astype(jnp.bfloat16)
        .reshape(tok_rows, 3, seq_count, head_width)
    )
    heads = lax.all_to_all(qkv, "seq", split_axis=2, concat_axis=0, tiled=True).reshape(
        group_rows, 3, head_width
    )
    pair = jnp.concatenate([heads[:, 1], heads[:, 2]], axis=1)
    window = padded(pair, (("fsdp", 0),), group_rows)
    query_heads = heads[:, 0].reshape(group_rows, head_count, HDIM).transpose(1, 0, 2)
    key_heads = window[:, :head_width].reshape(window_rows, head_count, HDIM).transpose(1, 0, 2)
    value_heads = window[:, head_width:].reshape(window_rows, head_count, HDIM).transpose(1, 0, 2)

    def masked_scores(query_block, key_all, start_row):
        scores = right_dot(query_block, key_all) * 0.125
        same = query_doc[start_row : start_row + block_rows, None] == key_doc[None, :]
        return jnp.where(same, scores, -1e30)

    def head_forward(operands):
        query_one, key_one, value_one, table = operands
        scores = masked_scores(query_one, key_one, 0)
        row_top = jnp.max(scores, axis=1, keepdims=True)
        weights = jnp.exp(scores - row_top)
        row_total = jnp.sum(weights, axis=1, keepdims=True)
        lookup = lookup_of(table, query_hot, key_hot)
        mixed = (weights / row_total * lookup).astype(jnp.bfloat16)
        outputs = [plain_dot(mixed, value_one)]
        totals = [row_top + jnp.log(row_total)]
        return (jnp.concatenate(outputs, axis=0), jnp.concatenate(totals, axis=0))

    context, log_totals = lax.map(head_forward, (query_heads, key_heads, value_heads, smooth_gate))
    context_low = context.transpose(1, 0, 2).reshape(group_rows, 1, head_width).astype(jnp.bfloat16)
    context_tok = lax.all_to_all(
        context_low, "seq", split_axis=0, concat_axis=1, tiled=True
    ).reshape(tok_rows, D)
    saved = token_forward(
        tokens, context_tok, full_out, full_up, full_down, full_biases, full_gains, full_bias_up
    )
    layer_out = layer_norm(saved[5], gain_rows[1], small[5]).astype(jnp.bfloat16)
    again = (
        lax.all_gather(projection_matrix_triple, ("seq", "fsdp"), axis=0, tiled=True),
        lax.all_gather(merge_matrix, ("seq", "fsdp"), axis=0, tiled=True),
        lax.all_gather(widen_matrix, ("seq", "fsdp"), axis=0, tiled=True),
        lax.all_gather(shrink_matrix, ("seq", "fsdp"), axis=0, tiled=True),
        lax.all_gather(offsets_turned, ("seq", "fsdp"), axis=0, tiled=True),
        lax.all_gather(gains_turned, ("seq", "fsdp"), axis=0, tiled=True),
        lax.all_gather(widen_offset, ("seq", "fsdp"), axis=0, tiled=True),
    )
    back_qkv, back_out, back_up, back_down = (again[0], again[1], again[2], again[3])
    hidden_one, normed, normed_low, up, act_low, hidden_two = token_forward(
        tokens, context_tok, again[1], again[2], again[3], again[4].T, again[5].T, again[6]
    )
    out_cot = result_cotangent.reshape(tok_rows, D).astype(jnp.float32)
    _, norm_two_pull = jax.vjp(layer_norm, hidden_two, gain_rows[1], small[5])
    grad_two, gain_two, shift_two = norm_two_pull(out_cot)
    down_low = grad_two.astype(jnp.bfloat16)
    grad_w_down = left_dot(act_low, down_low)
    grad_down_bias = jnp.sum(down_low.astype(jnp.float32), axis=0)
    _, gelu_pull = jax.vjp(partial(jax.nn.gelu, approximate=False), up)
    up_low = gelu_pull(right_dot(down_low, back_down))[0].astype(jnp.bfloat16)
    grad_w_up = left_dot(normed_low, up_low)
    grad_bias_up = jnp.sum(up_low.astype(jnp.float32), axis=0)
    grad_normed = grad_two + right_dot(up_low, back_up)
    _, norm_one_pull = jax.vjp(layer_norm, hidden_one, gain_rows[0], small[4])
    grad_one, gain_one, shift_one = norm_one_pull(grad_normed)
    attn_low = grad_one.astype(jnp.bfloat16)
    grad_w_out = left_dot(context_tok, attn_low)
    grad_out_bias = jnp.sum(attn_low.astype(jnp.float32), axis=0)
    context_grad = (
        right_dot(attn_low, back_out).astype(jnp.bfloat16).reshape(tok_rows, seq_count, head_width)
    )
    grad_heads = (
        lax.all_to_all(context_grad, "seq", split_axis=1, concat_axis=0, tiled=True)
        .reshape(group_rows, head_count, HDIM)
        .transpose(1, 0, 2)
    )

    def head_backward(operands):
        query_one, key_one, value_one, table, grad_head, total_one = operands
        key_grad = jnp.zeros((window_rows, HDIM), jnp.float32)
        value_grad = jnp.zeros((window_rows, HDIM), jnp.float32)
        table_grad = jnp.zeros((MPOS, MPOS), jnp.float32)
        probs = jnp.exp(masked_scores(query_one, key_one, 0) - total_one[0:block_rows])
        lookup = lookup_of(table, query_hot, key_hot)
        mixed = (probs * lookup).astype(jnp.bfloat16)
        mixed_grad = right_dot(grad_head, value_one)
        lookup_grad = mixed_grad * probs
        columns = jax.ops.segment_sum(lookup_grad.T, key_pos, num_segments=MPOS)
        table_grad = table_grad + jax.ops.segment_sum(columns.T, query_pos, num_segments=MPOS)
        prob_grad = mixed_grad * lookup
        delta = jnp.sum(prob_grad * probs, axis=1, keepdims=True)
        score_low = (probs * (prob_grad - delta)).astype(jnp.bfloat16)
        query_grads = [plain_dot(score_low, key_one) * 0.125]
        key_grad = key_grad + left_dot(score_low, query_one) * 0.125
        value_grad = value_grad + left_dot(mixed, grad_head)
        deltas = [delta]
        return (
            jnp.concatenate(query_grads, axis=0),
            key_grad,
            value_grad,
            table_grad,
            jnp.concatenate(deltas, axis=0),
        )

    query_grad, key_grad, value_grad, table_grad, row_deltas = lax.map(
        head_backward, (query_heads, key_heads, value_heads, smooth_gate, grad_heads, log_totals)
    )
    key_flat = key_grad.transpose(1, 0, 2)
    value_flat = value_grad.transpose(1, 0, 2)
    window_grad = jnp.concatenate(
        [key_flat.reshape(window_rows, head_width), value_flat.reshape(window_rows, head_width)],
        axis=1,
    )
    from_right = shifted(as_sent(window_grad[:group_rows]), "fsdp", -1)
    from_left = shifted(as_sent(window_grad[2 * group_rows :]), "fsdp", 1)
    own_grad = window_grad[group_rows : 2 * group_rows] + from_right + from_left
    query_flat = query_grad.transpose(1, 0, 2).reshape(group_rows, head_width)
    qkv_grad = (
        jnp.stack([query_flat, own_grad[:, :head_width], own_grad[:, head_width:]], axis=1)
        .astype(jnp.bfloat16)
        .reshape(group_rows, 3, 1, head_width)
    )
    token_grad = lax.all_to_all(qkv_grad, "seq", split_axis=0, concat_axis=2, tiled=True).reshape(
        tok_rows, 3 * D
    )
    grad_w_qkv = left_dot(tokens, token_grad)
    column_sums = jnp.sum(token_grad.astype(jnp.float32), axis=0)
    input_grad = grad_one + right_dot(token_grad, back_qkv)
    grad_small = jnp.stack(
        [
            column_sums[:D],
            column_sums[2 * D :],
            grad_out_bias,
            grad_down_bias,
            shift_one,
            shift_two,
        ],
        axis=1,
    )
    grad_gain_rows = jnp.stack([gain_one, gain_two], axis=1)
    summed = (
        lax.psum_scatter(grad_w_qkv, ("seq", "fsdp"), scatter_dimension=0, tiled=True),
        lax.psum_scatter(grad_w_out, ("seq", "fsdp"), scatter_dimension=0, tiled=True),
        lax.psum_scatter(grad_w_up, ("seq", "fsdp"), scatter_dimension=0, tiled=True),
        lax.psum_scatter(grad_w_down, ("seq", "fsdp"), scatter_dimension=0, tiled=True),
        lax.psum_scatter(grad_small, ("seq", "fsdp"), scatter_dimension=0, tiled=True),
        lax.psum_scatter(grad_gain_rows, ("seq", "fsdp"), scatter_dimension=0, tiled=True),
        lax.psum_scatter(grad_bias_up, ("seq", "fsdp"), scatter_dimension=0, tiled=True),
    )
    relaxed_mask_total = lax.psum_scatter(table_grad, "fsdp", scatter_dimension=1, tiled=True)
    mask_logit_gradient = (
        relaxed_mask_total
        * relaxed_mask_rows
        * (1.0 - relaxed_mask_rows)
        / softening_scale[:, None, None]
    )
    return (
        layer_out.reshape(1, tok_rows, D),
        input_grad.reshape(1, tok_rows, D),
        summed[0],
        summed[1],
        summed[2],
        summed[3],
        summed[4].T,
        summed[5].T,
        summed[6],
        mask_logit_gradient,
    )


def solution(mesh):
    return jax.shard_map(
        per_device,
        mesh=mesh,
        in_specs=(
            P("fsdp", "seq", None),
            P(("seq", "fsdp"), None),
            P(("seq", "fsdp"), None),
            P(("seq", "fsdp"), None),
            P(("seq", "fsdp"), None),
            P(None, ("seq", "fsdp")),
            P(None, ("seq", "fsdp")),
            P(("seq", "fsdp")),
            P("seq", "fsdp", None),
            P("seq", "fsdp", None),
            P("seq"),
            P(),
            P("fsdp", "seq", None),
        ),
        out_specs=(
            P("fsdp", "seq", None),
            P("fsdp", "seq", None),
            P(("seq", "fsdp"), None),
            P(("seq", "fsdp"), None),
            P(("seq", "fsdp"), None),
            P(("seq", "fsdp"), None),
            P(None, ("seq", "fsdp")),
            P(None, ("seq", "fsdp")),
            P(("seq", "fsdp")),
            P("seq", "fsdp", None),
        ),
        check_vma=False,
    )
```

profile of v0, /device:TPU:0, one launch (start us, length us, event | category | flops | bytes accessed | tf_op | source)
XLA Modules:
  0.0 1193.1 jit_solution(11110227320052372935)
XLA Ops:
  11.4 43.7 %all-gather = bf16[32,24,6]{1,2,0:T(8,128)(2,1)S(1)} all-gather(bf16[1,24,6]{1,2,0:T(8,128)(2,1)} %bitcast.285), channel_id=1, replica_groups=mesh['seq'=2,'fsdp'=16] {'seq','fsdp'}, dimensions={0}, use_global_device_ids=true | all-gather | bytes 9504 | tf_op jit(solution)/shard_map/all_gather | solution.py:135
  56.1 17.5 %all-gather.8.cloned.1.call-done = bf16[768,2304]{1,0:T(8,128)(2,1)} async-done(((bf16[24,2304]{1,0:T(8,128)(2,1)}), bf16[768,2304]{1,0:T(8,128)(2,1)}) %all-gather.8.cloned.1.call-update) | async-done | bytes 3538960 | tf_op jit(solution)/shard_map/all_gather | solution.py:131
  82.9 14.8 %all-to-all-done = bf16[256,3,2,384]{3,0,1,2:T(8,128)(2,1)S(1)} async-done(((bf16[256,3,2,384]{3,0,1,2:T(8,128)(2,1)}), bf16[256,3,2,384]{3,0,1,2:T(8,128)(2,1)S(1)}, u32[]{:S(2)}, u32[]{:S(2)}) %all-to-all-start) | async-done | bytes 1179680 | tf_op jit(solution)/shard_map/all_to_all | solution.py:172
  112.7 20.3 %all-gather.10.cloned.1.call-done = bf16[6,512,512]{2,1,0:T(8,128)(2,1)} async-done(((bf16[6,32,512]{2,1,0:T(8,128)(2,1)}), bf16[6,512,512]{2,1,0:T(8,128)(2,1)}) %all-gather.10.cloned.1.call-update) | async-done | bytes 3145744 | tf_op jit(solution)/shard_map/all_gather | solution.py:148
  133.0 59.6 %while.31 = (s32[]{:T(128)}, bf16[6,512,64]{1,2,0:T(8,128)(2,1)S(1)}, f32[6,512,1]{1,2,0:T(1,128)}, s32[512]{0:T(512)S(1)}, s32[1536]{0:T(1024)S(1)}, /*index=5*...) while((s32[]{:T(128)}, ...), condition=%wide.region_8.9_spmd.clone, body=%wide.region_5.8_spmd.clone.sunk | while | flops 1285291520 | bytes 12099717 | solution.py:198
  199.0 42.5 %all-reduce = bf16[3072]{0:T(1024)(128)(2,1)S(1)} all-reduce(bf16[3072]{0:T(1024)(128)(2,1)S(1)} %dynamic-update-slice), channel_id=1, replica_groups=mesh['seq'=2,'fsdp'=16] {'seq','fsdp'}, use_global_device_ids=true, to_apply=%add | all-reduce | flops 3072 | bytes 12288
  241.5 39.9 %all-gather.1 = bf16[32,24,2]{1,2,0:T(2,128)(2,1)S(1)} all-gather(bf16[1,24,2]{1,2,0:T(2,128)(2,1)S(1)} %bitcast.287), channel_id=1, replica_groups=mesh['seq'=2,'fsdp'=16] {'seq','fsdp'}, dimensions={0}, use_global_device_ids=true | all-gather | bytes 3168 | tf_op jit(solution)/shard_map/all_gather | solution.py:136
  285.0 11.4 multiply_convert_fusion.3
  296.4 23.1 %all-gather.16.cloned.1.call-done = bf16[3072,768]{1,0:T(8,128)(2,1)} async-done(((bf16[96,768]{1,0:T(8,128)(2,1)}), bf16[3072,768]{1,0:T(8,128)(2,1)}) %all-gather.16.cloned.1.call-update) | async-done | bytes 4718608 | tf_op jit(solution)/shard_map/all_gather | solution.py:134
  338.8 7.2 all-to-all-done.2
  348.2 241.1 %while.32 = (s32[]{:T(128)}, bf16[6,512,64]{1,2,0:T(8,128)(2,1)}, f32[6,1536,64]{1,2,0:T(8,128)}, f32[6,1536,64]{1,2,0:T(8,128)}, f32[6,512,512]{2,1,0:T(8,128)}...) while((s32[]{:T(128)}, bf16[6,512,64]{1,2,0:T(8,128)(2,1)}, ...), condition=%wide.region_21.22_spmd.clone.clone, body=%wide.region_17.21_spmd.clone.clone.sunk | while | flops 1597898240 | bytes 73859280 | solution.py:272
  350.7 4.7 fusion.210
  372.6 10.5 scatter_custom_fusion.14
  390.8 4.7 fusion.210
  412.7 10.5 scatter_custom_fusion.14
  430.9 4.7 fusion.210
  452.8 10.5 scatter_custom_fusion.14
  471.0 4.6 fusion.210
  492.9 10.5 scatter_custom_fusion.14
  511.1 4.7 fusion.210
  533.1 10.5 scatter_custom_fusion.14
  551.3 4.6 fusion.210
  573.3 10.5 scatter_custom_fusion.14
  604.7 14.7 %all_to_all.60 = bf16[512,3,1,384]{3,1,2,0:T(4,128)(2,1)S(1)} all-to-all(bf16[512,3,1,384]{3,1,2,0:T(4,128)(2,1)S(1)} %copy.191), channel_id=1, replica_groups=mesh['seq'=2,'fsdp'=16] {'seq'}, dimensions={0} | all-to-all | bytes 2359296 | tf_op jit(solution)/shard_map/all_to_all | solution.py:290
  624.3 8.0 copy.196
  633.5 6.6 fusion.126
  641.1 6.5 fusion.139
  649.2 56.1 %all-reduce.4 = (f32[768,6]{0,1:T(8,128)S(1)}, f32[768,2]{0,1:T(2,128)S(1)}, f32[3072]{0:T(1024)S(1)}) all-reduce(f32[768,6]{0,1:T(8,128)S(1)} %stack.51, f32[768,2]{0,1:T(2,128)S(1)} %pad_maximum_fusion.5, f32[3072]{0:T(1024)S(1)} %copy-done.32), channel_id=6, replica_groups=mesh['seq'=2,'fsdp'=16] {'seq','fsdp'}, use_global_device_ids=true, to_apply=%region_31.32.clone | all-reduce | flops 9216 | bytes 73728
  713.4 64.1 %reduce-scatter.10.cloned.1.call-done = f32[24,768]{1,0:T(8,128)} async-done(((f32[768,768]{1,0:T(8,128)}), f32[24,768]{1,0:T(8,128)}) %reduce-scatter.10.cloned.1.call-update) | async-done | bytes 73744 | tf_op jit(solution)/shard_map/reduce_scatter | solution.py:310
  777.5 124.9 %reduce-scatter.18.cloned.1.call-done = f32[24,2304]{1,0:T(8,128)} async-done(((f32[768,2304]{1,0:T(8,128)}), f32[24,2304]{1,0:T(8,128)}) %reduce-scatter.18.cloned.1.call-update) | async-done | bytes 221200
  902.3 141.9 %reduce-scatter.12.cloned.1.call-done = f32[24,3072]{1,0:T(8,128)} async-done(((f32[768,3072]{1,0:T(8,128)}), f32[24,3072]{1,0:T(8,128)}) %reduce-scatter.12.cloned.1.call-update) | async-done | bytes 294928 | tf_op jit(solution)/shard_map/reduce_scatter | solution.py:311
  1044.2 141.8 %reduce-scatter.14.cloned.1.call-done = f32[96,768]{1,0:T(8,128)} async-done(((f32[3072,768]{1,0:T(8,128)}), f32[96,768]{1,0:T(8,128)}) %reduce-scatter.14.cloned.1.call-update) | async-done | bytes 294928 | tf_op jit(solution)/shard_map/reduce_scatter | solution.py:312
  (353 shorter events, 301.3 us)
Async XLA Ops:
  7.2 66.5 %all-gather.8.cloned.1.call-start = ((), (), s32[]{:S(2)}) async-start(), calls=%async_computation.9 | async-start | bytes 3649536 | tf_op jit(solution)/shard_map/all_gather | solution.py:131
  7.9 125.1 %all-gather.10.cloned.1.call-start = ((), (), s32[]{:S(2)}) async-start(), calls=%async_computation.10 | async-start | bytes 3342336 | tf_op jit(solution)/shard_map/all_gather | solution.py:148
  10.1 272.7 %all-gather.12.cloned.1.call-start = ((), (), s32[]{:S(2)}) async-start(), calls=%async_computation.11 | async-start | bytes 1216512 | tf_op jit(solution)/shard_map/all_gather | solution.py:132
  10.8 274.2 %all-gather.14.cloned.1.call-start = ((), (), s32[]{:S(2)}) async-start(), calls=%async_computation.12 | async-start | bytes 4866048 | tf_op jit(solution)/shard_map/all_gather | solution.py:133
  78.4 19.3 %all-to-all-start = ((bf16[256,3,2,384]{3,0,1,2:T(8,128)(2,1)}), bf16[256,3,2,384]{3,0,1,2:T(8,128)(2,1)S(1)}, u32[]{:S(2)}, u32[]{:S(2)}) async-start(bf16[256,3,2,384]{3,0,1,2:T(8,128)(2,1)} %copy.173), calls=%async_computation | async-start | bytes 2359296 | tf_op jit(solution)/shard_map/all_to_all | solution.py:172
  82.0 237.5 %all-gather.16.cloned.1.call-start = ((), (), s32[]{:S(2)}) async-start(), calls=%async_computation.13 | async-start | bytes 4866048 | tf_op jit(solution)/shard_map/all_gather | solution.py:134
  99.0 7.2 collective-permute-start.1
  100.2 5.9 collective-permute-start
  192.6 48.8 %copy-start.40 = (bf16[2,24]{1,0:T(2,128)(2,1)S(1)}, bf16[2,24]{1,0:T(2,128)(2,1)}, u32[]{:S(2)}) copy-start(bf16[2,24]{1,0:T(2,128)(2,1)} %param.23) | copy-start | bytes 292
  193.2 89.7 %copy-start.14 = (bf16[1,256,768]{2,1,0:T(8,128)(2,1)S(1)}, bf16[1,256,768]{2,1,0:T(8,128)(2,1)}, u32[]{:S(2)}) copy-start(bf16[1,256,768]{2,1,0:T(8,128)(2,1)} %param.17) | copy-start | bytes 1179652
  193.2 89.7 %copy-start.29 = (f32[768]{0:T(1024)S(1)}, f32[768]{0:T(1024)}, u32[]{:S(2)}) copy-start(f32[768]{0:T(1024)} %get-tuple-element.537) | copy-start | bytes 9220
  195.2 86.5 %all-to-all-start.1 = ((bf16[2,2,49152]{2,1,0:T(2,128)(2,1)}), bf16[2,2,49152]{2,1,0:T(2,128)(2,1)S(1)}, u32[]{:S(2)}, u32[]{:S(2)}) async-start(bf16[2,2,49152]{2,1,0:T(2,128)(2,1)} %reshape.362), calls=%async_computation.1 | async-start | bytes 786432 | tf_op jit(solution)/shard_map/all_to_all | solution.py:200
  281.7 50.1 %copy-start.19 = (f32[768]{0:T(1024)}, f32[768]{0:T(1024)S(1)}, u32[]{:S(2)}) copy-start(f32[768]{0:T(1024)S(1)} %get-tuple-element.543) | copy-start | bytes 9220
  284.7 47.0 %copy-start.1 = (f32[256,768]{1,0:T(8,128)}, f32[256,768]{1,0:T(8,128)S(1)}, u32[]{:S(2)}) copy-start(f32[256,768]{1,0:T(8,128)S(1)} %get-tuple-element.633) | copy-start | bytes 2359300
  284.7 47.0 %copy-start.23 = (f32[256]{0:T(256)}, f32[256]{0:T(256)S(1)}, u32[]{:S(2)}) copy-start(f32[256]{0:T(256)S(1)} %broadcast_multiply_fusion.1) | copy-start | bytes 3076
  285.0 46.8 %copy-start.30 = (f32[256]{0:T(256)}, f32[256]{0:T(256)S(1)}, u32[]{:S(2)}) copy-start(f32[256]{0:T(256)S(1)} %fusion.124) | copy-start | bytes 3076
  285.0 34.5 %copy-start.35 = (f32[768]{0:T(1024)S(1)}, f32[768]{0:T(1024)}, u32[]{:S(2)}) copy-start(f32[768]{0:T(1024)} %get-tuple-element.535) | copy-start | bytes 9220
  296.4 27.1 %copy-start.11 = (bf16[256,3072]{1,0:T(8,128)(2,1)}, bf16[256,3072]{1,0:T(8,128)(2,1)S(1)}, u32[]{:S(2)}) copy-start(bf16[256,3072]{1,0:T(8,128)(2,1)S(1)} %get-tuple-element.613) | copy-start | bytes 4718596
  319.6 7.1 slice-start.2
  319.6 7.1 slice-start.3
  332.1 15.3 %copy-start.10 = (f32[256,768]{1,0:T(8,128)}, f32[256,768]{1,0:T(8,128)S(1)}, u32[]{:S(2)}) copy-start(f32[256,768]{1,0:T(8,128)S(1)} %get-tuple-element.610) | copy-start | bytes 2359300
  332.1 15.3 %copy-start.36 = (f32[256]{0:T(256)}, f32[256]{0:T(256)S(1)}, u32[]{:S(2)}) copy-start(f32[256]{0:T(256)S(1)} %negate_multiply_fusion.1) | copy-start | bytes 3076
  335.2 10.7 all-to-all-start.2
  338.7 372.8 %reduce-scatter.16.cloned.1.call-start = ((), (), s32[]{:S(2)}) async-start(), calls=%async_computation.17 | async-start | bytes 6684672 | tf_op jit(solution)/shard_map/reduce_scatter | solution.py:317
  589.4 188.1 %reduce-scatter.10.cloned.1.call-start = ((), (), s32[]{:S(2)}) async-start(), calls=%async_computation.14 | async-start | bytes 2433024 | tf_op jit(solution)/shard_map/reduce_scatter | solution.py:310
  592.3 310.1 %reduce-scatter.18.cloned.1.call-start = ((), (), s32[]{:S(2)}) async-start(), calls=%async_computation.18 | async-start | bytes 7299072
  594.5 8.1 copy-start.4
  594.6 3.9 collective-permute-start.3
  596.3 6.4 collective-permute-start.2
  632.4 411.8 %reduce-scatter.12.cloned.1.call-start = ((), (), s32[]{:S(2)}) async-start(), calls=%async_computation.15 | async-start | bytes 9732096 | tf_op jit(solution)/shard_map/reduce_scatter | solution.py:311
  640.2 545.8 %reduce-scatter.14.cloned.1.call-start = ((), (), s32[]{:S(2)}) async-start(), calls=%async_computation.16 | async-start | bytes 9732096 | tf_op jit(solution)/shard_map/reduce_scatter | solution.py:312
  647.7 59.5 %copy-start.37 = (f32[256]{0:T(256)S(1)}, f32[256]{0:T(256)}, u32[]{:S(2)}) copy-start(f32[256]{0:T(256)} %copy-done.36) | copy-start | bytes 3076
  (38 other events, 111.2 us)
Sparse Core Ops, SparseCore 0:
  10.9 62.6 all-gather.7
  76.4 56.5 all-gather.9
  135.9 52.8 all-gather.11
  191.5 63.1 all-gather.13
  257.4 62.0 all-gather.15
  589.5 83.3 reduce-scatter.15
  678.7 98.7 reduce-scatter.9
  783.7 118.5 reduce-scatter.17
  908.8 135.3 reduce-scatter.11
  1050.5 135.3 reduce-scatter.13
where the time goes:
time: 1200 us; the launch traced here: 1190 us
  waiting for transfers between devices  563 us (47%)
  blocking collectives  197 us (16%)
  matrix products  194 us (16%)
  other arithmetic  133 us (11%)
  local copies, waits for them, and re-layouts  71.7 us (6%)
  starting transfers between devices  18.3 us (2%)
  between operations  15.3 us (1%)
    reduce_scatter x1, waiting for transfers between devices, per_device(): lax.psum_scatter(grad_w_up, ('seq', 'fsdp'), scatter_dimension=0, tiled=T...  142 us
    reduce_scatter x1, waiting for transfers between devices, per_device(): lax.psum_scatter(grad_w_down, ('seq', 'fsdp'), scatter_dimension=0, tiled...  142 us
    unnamed x11, waiting for transfers between devices  127 us
    unnamed x2, blocking collectives  98.6 us
    dot_general x28, matrix products, right_dot(): lax.dot_general(left, right, (((1,), (1,)), ((), ())), preferred_element_...  78 us
    dot_general x22, matrix products, plain_dot(): return jnp.dot(left, right, preferred_element_type=jnp.float32)  69.2 us
    reduce_scatter x1, waiting for transfers between devices, per_device(): lax.psum_scatter(grad_w_out, ('seq', 'fsdp'), scatter_dimension=0, tiled=...  64.1 us
    scatter-add x6, other arithmetic, head_backward(): columns = jax.ops.segment_sum(lookup_grad.T, key_pos, num_segments=MPOS)  63 us
  transfers between devices with their start and end apart: 17, of which 11 were waited for; matrix products, arithmetic and copies ran while one was open for 11% of the time, Pallas kernels for 0%

commit v1 on v0

v1 whole, which is shorter than its diff:
```python
from functools import partial

import jax
import jax.numpy as jnp
from jax import lax
from jax.experimental import pallas as pl
from jax.experimental.pallas import tpu as pltpu
from jax.sharding import PartitionSpec as P

D = 768
FOCUS_COUNT = 12
HDIM = 64
MPOS = 512
EPS = 1e-05
BLOCK = 512
PAIR = 128
TILE = 128
PIECE = 32
BOTH = ("seq", "fsdp")
BF = jnp.bfloat16
F32 = jnp.float32


def layer_norm(values, gain, shift):
    center = values - jnp.mean(values, axis=-1, keepdims=True)
    spread = jnp.mean(center * center, axis=-1, keepdims=True)
    return center * lax.rsqrt(spread + EPS) * gain + shift


def plain_dot(left, right):
    return jnp.dot(left, right, preferred_element_type=F32)


def left_dot(left, right):
    return lax.dot_general(left, right, (((0,), (0,)), ((), ())), preferred_element_type=F32)


def right_dot(left, right):
    return lax.dot_general(left, right, (((1,), (1,)), ((), ())), preferred_element_type=F32)


def two_heads(rows):
    lane = lax.broadcasted_iota(jnp.int32, rows.shape, 1)
    zero = jnp.zeros_like(rows)
    return jnp.concatenate(
        [jnp.where(lane < HDIM, rows, zero), jnp.where(lane < HDIM, zero, rows)], axis=0
    ).astype(BF)


def one_row_set(pairs):
    half = pairs.shape[0] // 2
    lane = lax.broadcasted_iota(jnp.int32, (half, pairs.shape[1]), 1)
    return jnp.where(lane < HDIM, pairs[:half], pairs[half:])


def for_documents(extent_ref, info_ref, visit):
    first = info_ref[0]

    def step(index, begin):
        length = extent_ref[index]
        finish = begin + length

        @pl.when((begin < first + BLOCK) & (finish > first))
        def _():
            visit(begin - first + BLOCK, length)

        return finish

    lax.fori_loop(0, extent_ref.shape[0], step, jnp.int32(0))


def table_rows(table_ref, info_ref, tile):
    parts = []
    for head in range(2):
        for piece in range(TILE // PIECE):
            where = info_ref[1 + tile * (TILE // PIECE) + piece]
            parts.append(table_ref[where, head])
    return jnp.concatenate(parts, axis=0).astype(F32)


def weights_of(queries, keys, length):
    scores = right_dot(queries, keys)
    column = lax.broadcasted_iota(jnp.int32, scores.shape, 1)
    scores = jnp.where(column < length, scores, -1e30)
    weights = jnp.exp(scores - jnp.max(scores, axis=1, keepdims=True))
    return weights, jnp.sum(weights, axis=1, keepdims=True)


def fill_window(window, low, own, high):
    window[0:BLOCK, :] = low[...].astype(F32)
    window[BLOCK : 2 * BLOCK, :] = own[...].astype(F32)
    window[2 * BLOCK : 3 * BLOCK, :] = high[...].astype(F32)


def fill_middle(window, own, scale=None):
    value = own[...].astype(F32)
    zero = jnp.zeros((BLOCK, PAIR), F32)
    window[0:BLOCK, :] = zero
    window[BLOCK : 2 * BLOCK, :] = value if scale is None else value * scale
    window[2 * BLOCK : 3 * BLOCK, :] = zero


def forward_kernel(
    extent_ref, info_ref, q_ref, k_ref, v_ref, lk_ref, lv_ref, hk_ref, hv_ref, table_ref, out_ref,
    q_win, k_win, v_win, o_win, k_doc, v_doc,
):
    fill_middle(q_win, q_ref, 0.125)
    fill_window(k_win, lk_ref, k_ref, hk_ref)
    fill_window(v_win, lv_ref, v_ref, hv_ref)

    def visit(offset, length):
        k_doc[...] = k_win[pl.ds(offset, MPOS), :].astype(BF)
        v_doc[...] = v_win[pl.ds(offset, MPOS), :].astype(BF)
        start = jnp.maximum(0, BLOCK - offset)
        finish = jnp.minimum(length, 2 * BLOCK - offset)

        def tile(index, carry):
            at = pl.ds(offset + index * TILE, TILE)
            weights, total = weights_of(two_heads(q_win[at, :]), k_doc[...], length)
            mixed = (weights * table_rows(table_ref, info_ref, index)).astype(BF)
            o_win[at, :] = one_row_set(plain_dot(mixed, v_doc[...]) / total)
            return carry

        lax.fori_loop(start // TILE, (finish + TILE - 1) // TILE, tile, 0)

    for_documents(extent_ref, info_ref, visit)
    out_ref[...] = o_win[BLOCK : 2 * BLOCK, :].astype(BF)


def backward_kernel(
    extent_ref, info_ref, q_ref, k_ref, v_ref, lk_ref, lv_ref, hk_ref, hv_ref, table_ref, g_ref,
    dq_ref, dk_ref, dv_ref, dt_ref,
    q_win, k_win, v_win, g_win, dq_win, dk_win, dv_win, dt_all, k_doc, v_doc, dk_doc, dv_doc,
):
    fill_middle(q_win, q_ref, 0.125)
    fill_middle(g_win, g_ref)
    fill_window(k_win, lk_ref, k_ref, hk_ref)
    fill_window(v_win, lv_ref, v_ref, hv_ref)
    dk_win[...] = jnp.zeros_like(dk_win)
    dv_win[...] = jnp.zeros_like(dv_win)
    dt_all[...] = jnp.zeros_like(dt_all)

    def visit(offset, length):
        k_doc[...] = k_win[pl.ds(offset, MPOS), :].astype(BF)
        v_doc[...] = v_win[pl.ds(offset, MPOS), :].astype(BF)
        dk_doc[...] = jnp.zeros_like(dk_doc)
        dv_doc[...] = jnp.zeros_like(dv_doc)
        start = jnp.maximum(0, BLOCK - offset)
        finish = jnp.minimum(length, 2 * BLOCK - offset)

        def tile(index, carry):
            at = pl.ds(offset + index * TILE, TILE)
            queries = two_heads(q_win[at, :])
            grads = two_heads(g_win[at, :])
            weights, total = weights_of(queries, k_doc[...], length)
            place = lax.broadcasted_iota(jnp.int32, (2, TILE, 1), 1).reshape(2 * TILE, 1)
            place = place + index * TILE
            probs = weights * jnp.where((place >= start) & (place < finish), 1.0 / total, 0.0)
            lookup = table_rows(table_ref, info_ref, index)
            mixed_grad = right_dot(grads, v_doc[...])
            mixed = probs * lookup
            lookup_grad = mixed_grad * probs
            delta = jnp.sum(lookup_grad * lookup, axis=1, keepdims=True)
            score_low = (probs * (mixed_grad * lookup - delta)).astype(BF)
            rows = pl.ds(pl.multiple_of(index * TILE, TILE), TILE)
            dt_all[0, rows, :] += lookup_grad[:TILE]
            dt_all[1, rows, :] += lookup_grad[TILE:]
            dq_win[at, :] = one_row_set(plain_dot(score_low, k_doc[...]) * 0.125)
            dk_doc[...] += left_dot(score_low, queries)
            dv_doc[...] += left_dot(mixed.astype(BF), grads)
            return carry

        lax.fori_loop(start // TILE, (finish + TILE - 1) // TILE, tile, 0)
        dk_win[pl.ds(offset, MPOS), :] = dk_doc[...]
        dv_win[pl.ds(offset, MPOS), :] = dv_doc[...]

    for_documents(extent_ref, info_ref, visit)
    dq_ref[...] = dq_win[BLOCK : 2 * BLOCK, :].astype(BF)
    dk_ref[...] = dk_win[...].astype(BF)
    dv_ref[...] = dv_win[...].astype(BF)
    dt_ref[...] = dt_all[...].astype(BF)


def attention_specs(steps):
    def column(shift):
        return pl.BlockSpec((BLOCK, PAIR), lambda i: (0, i + shift))

    smem = pl.BlockSpec(memory_space=pltpu.SMEM)
    return [smem, smem, column(0), column(steps), column(2 * steps)] + [
        column(0), column(steps), column(0), column(steps),
        pl.BlockSpec((MPOS // PIECE, 2, PIECE, MPOS), lambda i: (0, i, 0, 0)),
    ]


def window_scratch(count):
    return [pltpu.VMEM((3 * BLOCK, PAIR), F32) for _ in range(count)]


def attend(extents, info, qkv, low, high, table):
    steps = qkv.shape[1] // (3 * PAIR)
    return pl.pallas_call(
        forward_kernel,
        grid=(steps,),
        in_specs=attention_specs(steps),
        out_specs=pl.BlockSpec((BLOCK, PAIR), lambda i: (0, i)),
        out_shape=jax.ShapeDtypeStruct((BLOCK, steps * PAIR), BF),
        scratch_shapes=window_scratch(4) + [pltpu.VMEM((MPOS, PAIR), BF) for _ in range(2)],
        name="attend",
    )(extents, info, qkv, qkv, qkv, low, low, high, high, table)


def attend_back(extents, info, qkv, low, high, table, grads):
    steps = qkv.shape[1] // (3 * PAIR)
    narrow = pl.BlockSpec((BLOCK, PAIR), lambda i: (0, i))
    wide = pl.BlockSpec((3 * BLOCK, PAIR), lambda i: (0, i))
    return pl.pallas_call(
        backward_kernel,
        grid=(steps,),
        in_specs=attention_specs(steps) + [narrow],
        out_specs=[narrow, wide, wide, pl.BlockSpec((2, MPOS, MPOS), lambda i: (i, 0, 0))],
        out_shape=[
            jax.ShapeDtypeStruct((BLOCK, steps * PAIR), BF),
            jax.ShapeDtypeStruct((3 * BLOCK, steps * PAIR), BF),
            jax.ShapeDtypeStruct((3 * BLOCK, steps * PAIR), BF),
            jax.ShapeDtypeStruct((2 * steps, MPOS, MPOS), BF),
        ],
        scratch_shapes=window_scratch(7)
        + [pltpu.VMEM((2, MPOS, MPOS), F32)]
        + [pltpu.VMEM((MPOS, PAIR), BF) for _ in range(2)]
        + [pltpu.VMEM((MPOS, PAIR), F32) for _ in range(2)],
        name="attend_back",
    )(extents, info, qkv, qkv, qkv, low, low, high, high, table, grads)


def swapped(value):
    return lax.ppermute(value, "seq", [(0, 1), (1, 0)])


def crossed(value, bit):
    count = lax.axis_size("fsdp")
    return lax.ppermute(value, "fsdp", [(i, i ^ (1 << bit)) for i in range(count)])


def from_neighbour(value, steps):
    count = lax.axis_size("fsdp")
    leading, last = (max(0, -steps), min(count, count - steps))
    return lax.ppermute(value, "fsdp", [(i, i + steps) for i in range(leading, last)])


def in_order(mine, other, side, axis):
    return jnp.where(
        side == 0,
        jnp.concatenate([mine, other], axis=axis),
        jnp.concatenate([other, mine], axis=axis),
    )


def bits_of(count):
    return count.bit_length() - 1


def gathered(value):
    count = lax.axis_size("fsdp")
    inner = 4
    outer = count // inner
    far = [[a * inner + b for a in range(outer)] for b in range(inner)]
    near = [[a * inner + b for b in range(inner)] for a in range(outer)]
    value = lax.all_gather(value, "fsdp", axis=0, axis_index_groups=far)
    value = lax.all_gather(value, "fsdp", axis=0, axis_index_groups=near)
    return jnp.swapaxes(value, 0, 1).reshape((count,) + value.shape[2:])


def spread(value, own):
    count = lax.axis_size("fsdp")
    total = bits_of(count)
    order = list(range(total - 1, 1, -1)) + [1, 0]
    value = value[None]
    for bit in order:
        value = jnp.concatenate([value, crossed(value, bit)], axis=0)
    away = own ^ jnp.arange(count, dtype=jnp.int32)
    place = sum(((away >> bit) & 1) << rank for rank, bit in enumerate(order))
    return value, place


def summed_part(value, own, axis):
    count = lax.axis_size("fsdp")
    total = bits_of(count)
    shape = value.shape
    value = value.reshape(shape[:axis] + (2,) * total + shape[axis + 1 :])
    left = list(range(total - 1, -1, -1))
    for bit in [0, 1] + list(range(total - 1, 1, -1)):
        at = axis + left.index(bit)
        mine = (own >> bit) & 1
        keep = lax.dynamic_index_in_dim(value, mine, axis=at, keepdims=False)
        send = lax.dynamic_index_in_dim(value, 1 - mine, axis=at, keepdims=False)
        value = keep.astype(F32) + crossed(send.astype(BF), bit).astype(F32)
        left.remove(bit)
    return value


def per_device(
    incoming_state,
    projection_matrix_triple,
    merge_matrix,
    widen_matrix,
    shrink_matrix,
    offset_table,
    norm_scales,
    widen_offset,
    trainable_gate_scores,
    gate_perturbation,
    softening_scale,
    passage_extents,
    result_cotangent,
):
    tok_rows = incoming_state.shape[1]
    tokens = incoming_state.reshape(tok_rows, D)
    seq_count = lax.axis_size("seq")
    shards = lax.axis_size("fsdp")
    devices = seq_count * shards
    head_width = D // seq_count
    group_rows = tok_rows * seq_count
    rows = D // devices
    up_cols = widen_matrix.shape[1]
    blocks = up_cols // D
    side = lax.axis_index("seq")
    own = lax.axis_index("fsdp")

    small = jnp.concatenate([offset_table[2:].reshape(-1), norm_scales.reshape(-1), widen_offset])
    small_row = jnp.pad(small[None], ((0, 7), (0, D - small.shape[0])))
    pack = jnp.concatenate(
        [merge_matrix]
        + [widen_matrix[:, k * D : (k + 1) * D] for k in range(blocks)]
        + [shrink_matrix, small_row],
        axis=0,
    )
    everyone = lax.all_gather(pack, BOTH, axis=0)

    triple = projection_matrix_triple.reshape(rows, 3, seq_count, head_width)
    kept = lax.dynamic_index_in_dim(triple, side, 2, keepdims=False).reshape(rows, 3 * head_width)
    sent = lax.dynamic_index_in_dim(triple, 1 - side, 2, keepdims=False)
    other = swapped(sent.reshape(rows, 3 * head_width))
    block_tokens = in_order(tokens, swapped(tokens), side, 0)
    qv_bias = jnp.concatenate([offset_table[0], offset_table[1]])
    bias_row = jnp.pad(qv_bias[None], ((0, 7), (0, 3 * head_width - 2 * rows)))
    share = jnp.concatenate([in_order(kept, other, side, 0), bias_row], axis=0)
    shares = gathered(share)
    heads_matrix = (
        shares[:, : seq_count * rows]
        .reshape(shards, seq_count, rows, 3 * head_width)
        .swapaxes(0, 1)
        .reshape(D, 3 * head_width)
    )
    q_bias = shares[:, seq_count * rows, :rows].reshape(-1)
    v_bias = shares[:, seq_count * rows, rows : 2 * rows].reshape(-1)
    heads_bias = jnp.concatenate([q_bias, jnp.zeros_like(q_bias), v_bias]).astype(F32)

    relaxed_mask_rows = jax.nn.sigmoid(
        (trainable_gate_scores + gate_perturbation) / softening_scale[:, None, None]
    )
    pieces = MPOS // PIECE
    if relaxed_mask_rows.shape[1] == PIECE:
        table, place = spread(relaxed_mask_rows.astype(BF), own)
    else:
        table = lax.all_gather(relaxed_mask_rows.astype(BF), "fsdp", axis=1, tiled=True)
        table = table.reshape(table.shape[0], pieces, PIECE, MPOS).swapaxes(0, 1)
        place = jnp.arange(pieces, dtype=jnp.int32)
    info = jnp.concatenate([(own * group_rows)[None].astype(jnp.int32), place])

    qkv = (plain_dot(block_tokens, heads_matrix) + heads_bias).astype(BF)
    pair = qkv[:, head_width:]
    low = from_neighbour(pair, 1)
    high = from_neighbour(pair, -1)
    context = attend(passage_extents, info, qkv, low, high, table)

    def rows_of(value, which):
        return lax.dynamic_slice_in_dim(value, which * tok_rows, tok_rows, axis=0)

    context_tok = in_order(
        rows_of(context, side), swapped(rows_of(context, 1 - side)), side, 1
    )

    full_out = everyone[:, :rows].reshape(D, D)
    full_up = jnp.concatenate(
        [everyone[:, (k + 1) * rows : (k + 2) * rows].reshape(D, D) for k in range(blocks)], axis=1
    )
    at = (blocks + 1) * rows
    full_down = everyone[:, at : at + blocks * rows].reshape(up_cols, D)
    smalls = everyone[:, at + blocks * rows, : small.shape[0]].astype(F32)
    vectors = smalls[:, : 6 * rows].reshape(devices, 6, rows).swapaxes(0, 1).reshape(6, D)
    out_bias, down_bias, shift_a, shift_b, gain_a, gain_b = [vectors[k] for k in range(6)]
    up_bias = smalls[:, 6 * rows :].reshape(-1)

    hidden_one = tokens.astype(F32) + (plain_dot(context_tok, full_out) + out_bias)
    normed, norm_one_pull = jax.vjp(layer_norm, hidden_one, gain_a, shift_a)
    normed_low = normed.astype(BF)
    up = plain_dot(normed_low, full_up) + up_bias
    act, gelu_pull = jax.vjp(partial(jax.nn.gelu, approximate=False), up)
    act_low = act.astype(BF)
    hidden_two = normed + (plain_dot(act_low, full_down) + down_bias)
    out, norm_two_pull = jax.vjp(layer_norm, hidden_two, gain_b, shift_b)
    layer_out = out.astype(BF)

    out_cot = result_cotangent.reshape(tok_rows, D).astype(F32)
    grad_two, gain_two, shift_two = norm_two_pull(out_cot)
    down_low = grad_two.astype(BF)
    up_low = gelu_pull(right_dot(down_low, full_down))[0].astype(BF)
    grad_normed = grad_two + right_dot(up_low, full_up)
    grad_one, gain_one, shift_one = norm_one_pull(grad_normed)
    attn_low = grad_one.astype(BF)
    context_grad = right_dot(attn_low, full_out).astype(BF)

    def columns_of(value, which):
        return lax.dynamic_slice_in_dim(value, which * head_width, head_width, axis=1)

    grad_heads = in_order(
        columns_of(context_grad, side), swapped(columns_of(context_grad, 1 - side)), side, 0
    )

    def shares_of(value):
        return value.astype(BF).reshape(devices, -1, D)

    grad_w_down = left_dot(act_low, down_low)
    grad_w_up = left_dot(normed_low, up_low)
    grad_w_out = left_dot(context_tok, attn_low)
    sums = [
        jnp.sum(attn_low.astype(F32), axis=0),
        jnp.sum(down_low.astype(F32), axis=0),
        shift_one,
        shift_two,
        gain_one,
        gain_two,
        jnp.sum(up_low.astype(F32), axis=0),
    ]
    sum_row = jnp.concatenate([value.reshape(devices, -1) for value in sums], axis=1).astype(BF)
    sum_row = jnp.pad(sum_row[:, None], ((0, 0), (0, 7), (0, D - sum_row.shape[1])))
    grads = jnp.concatenate(
        [shares_of(grad_w_out)]
        + [shares_of(grad_w_up[:, k * D : (k + 1) * D]) for k in range(blocks)]
        + [shares_of(grad_w_down), sum_row],
        axis=1,
    )
    early = lax.psum_scatter(grads, BOTH, scatter_dimension=0)

    query_grad, key_grad, value_grad, table_grad = attend_back(
        passage_extents, info, qkv, low, high, table, grad_heads
    )
    window_grad = jnp.concatenate([key_grad, value_grad], axis=1)
    from_right = from_neighbour(window_grad[:group_rows], -1)
    from_left = from_neighbour(window_grad[2 * group_rows :], 1)
    pair_grad = (
        window_grad[group_rows : 2 * group_rows].astype(F32)
        + from_right.astype(F32)
        + from_left.astype(F32)
    ).astype(BF)
    heads_grad = jnp.concatenate([query_grad, pair_grad], axis=1)

    heads_matrix_grad = (
        left_dot(block_tokens, heads_grad)
        .astype(BF)
        .reshape(seq_count, shards, rows, 3 * head_width)
        .swapaxes(0, 1)
        .reshape(shards, seq_count * rows, 3 * head_width)
    )
    column_sums = jnp.sum(heads_grad.astype(F32), axis=0).astype(BF)
    qv_sums = jnp.concatenate(
        [
            column_sums[:head_width].reshape(shards, rows),
            column_sums[2 * head_width :].reshape(shards, rows),
        ],
        axis=1,
    )
    qv_row = jnp.pad(qv_sums[:, None], ((0, 0), (0, 7), (0, 3 * head_width - 2 * rows)))
    late = summed_part(jnp.concatenate([heads_matrix_grad, qv_row], axis=1), own, 0)
    late_rows = late[: seq_count * rows].reshape(seq_count, rows, 3 * head_width)
    late_mine = lax.dynamic_index_in_dim(late_rows, side, 0, keepdims=False)
    late_other = swapped(lax.dynamic_index_in_dim(late_rows, 1 - side, 0, keepdims=False).astype(BF))
    grad_w_qkv = in_order(
        late_mine.reshape(rows, 3, 1, head_width),
        late_other.astype(F32).reshape(rows, 3, 1, head_width),
        side,
        2,
    ).reshape(rows, 3 * D)
    qv_total = late[seq_count * rows, : 2 * rows].reshape(2, rows)

    partial_input = right_dot(heads_grad, heads_matrix)
    input_grad = (
        grad_one
        + rows_of(partial_input, side)
        + swapped(rows_of(partial_input, 1 - side).astype(BF)).astype(F32)
    )

    table_rows_each = MPOS // shards
    table_total = summed_part(
        table_grad.reshape(table_grad.shape[0], shards, table_rows_each, MPOS), own, 1
    )
    mask_logit_gradient = (
        table_total
        * relaxed_mask_rows
        * (1.0 - relaxed_mask_rows)
        / softening_scale[:, None, None]
    )
    early = early.astype(F32)
    totals = early[at + blocks * rows, : 6 * rows + blocks * rows]
    named = totals[: 6 * rows].reshape(6, rows)
    return (
        layer_out.reshape(1, tok_rows, D),
        input_grad.reshape(1, tok_rows, D),
        grad_w_qkv,
        early[:rows],
        jnp.concatenate([early[(k + 1) * rows : (k + 2) * rows] for k in range(blocks)], axis=1),
        early[at : at + blocks * rows],
        jnp.concatenate([qv_total, named[:4]], axis=0),
        named[4:6],
        totals[6 * rows :],
        mask_logit_gradient,
    )


def solution(mesh):
    return jax.shard_map(
        per_device,
        mesh=mesh,
        in_specs=(
            P("fsdp", "seq", None),
            P(("seq", "fsdp"), None),
            P(("seq", "fsdp"), None),
            P(("seq", "fsdp"), None),
            P(("seq", "fsdp"), None),
            P(None, ("seq", "fsdp")),
            P(None, ("seq", "fsdp")),
            P(("seq", "fsdp")),
            P("seq", "fsdp", None),
            P("seq", "fsdp", None),
            P("seq"),
            P(),
            P("fsdp", "seq", None),
        ),
        out_specs=(
            P("fsdp", "seq", None),
            P("fsdp", "seq", None),
            P(("seq", "fsdp"), None),
            P(("seq", "fsdp"), None),
            P(("seq", "fsdp"), None),
            P(("seq", "fsdp"), None),
            P(None, ("seq", "fsdp")),
            P(None, ("seq", "fsdp")),
            P(("seq", "fsdp")),
            P("seq", "fsdp", None),
        ),
        check_vma=False,
    )
```

time: 1200 us -> 392 us (0.33)
  waiting for transfers between devices: 563 us -> 150 us
  blocking collectives: 197 us -> 16.2 us
  matrix products: 194 us -> 33.7 us
  other arithmetic: 133 us -> 21.4 us
  starting transfers between devices: 18.3 us -> 54.9 us
  Pallas kernels: 0 us -> 32.2 us
    reduce_scatter x4 -> x1, waiting for transfers between devices: 348 us -> 4.44 us  [per_device(): early = lax.psum_scatter(grads, BOTH, scatter_dimension=0)]
    unnamed x11 -> x3, waiting for transfers between devices: 127 us -> 0.05 us
    ppermute x4 -> x22, waiting for transfers between devices: 4.98 us -> 113 us  [the longest x12 97.1 us: crossed(): lax.ppermute(value, 'fsdp', [(i, i ^ 1 << bit) for i in range(count)])]
    unnamed x2 -> x0, blocking collectives: 98.6 us -> none
    scatter-add x12 -> x0, other arithmetic: 86.7 us -> none  [the longest x6 63 us: head_backward(): columns = jax.ops.segment_sum(lookup_grad.T, key_pos, num_segments=MPOS)]
    dot_general x28 -> x4, matrix products: 78 us -> 8.66 us  [right_dot(): lax.dot_general(left, right, (((1,), (1,)), ((), ())), preferred_element_...]
    all_gather x2 -> x1, blocking collectives: 83.6 us -> 16.2 us  [gathered(): value = lax.all_gather(value, 'fsdp', axis=0, axis_index_groups=far)]
    dot_general x22 -> x4, matrix products: 69.2 us -> 14.3 us  [plain_dot(): return jnp.dot(left, right, preferred_element_type=F32)]
  transfers between devices with their start and end apart: 17 -> 25, of which waited for: 11 -> 15; matrix products, arithmetic and copies ran while one was open for 11% -> 17% of each run, Pallas kernels for 0% -> 8%
where the time goes in v1:
time: 392 us; the launch traced here: 391 us
  waiting for transfers between devices  150 us (38%)
  local copies, waits for them, and re-layouts  67.5 us (17%)
  starting transfers between devices  54.9 us (14%)
  matrix products  33.7 us (9%)
  Pallas kernels  32.2 us (8%)
  other arithmetic  21.4 us (5%)
  blocking collectives  16.2 us (4%)
  between operations  14.7 us (4%)
    ppermute x12, waiting for transfers between devices, crossed(): lax.ppermute(value, 'fsdp', [(i, i ^ 1 << bit) for i in range(count)])  97.1 us
    ppermute x12, starting transfers between devices, crossed(): lax.ppermute(value, 'fsdp', [(i, i ^ 1 << bit) for i in range(count)])  33 us
    all_gather x1, waiting for transfers between devices, per_device(): everyone = lax.all_gather(pack, BOTH, axis=0)  32.6 us
    unnamed x91, local copies, waits for them, and re-layouts  24.7 us
    pallas_call x1, Pallas kernels, attend_back(): pl.pallas_call(backward_kernel, grid=(steps,), in_specs=attention_specs(s...  20.5 us
    all_gather x1, blocking collectives, gathered(): value = lax.all_gather(value, 'fsdp', axis=0, axis_index_groups=far)  16.2 us
    ppermute x6, waiting for transfers between devices, swapped(): return lax.ppermute(value, 'seq', [(0, 1), (1, 0)])  14.7 us
    dot_general x4, matrix products, plain_dot(): return jnp.dot(left, right, preferred_element_type=F32)  14.3 us
  transfers between devices with their start and end apart: 25, of which 15 were waited for; matrix products, arithmetic and copies ran while one was open for 17% of the time, Pallas kernels for 8%

profile of v1, /device:TPU:0, one launch (start us, length us, event | category | flops | bytes accessed | tf_op | source)
XLA Modules:
  0.0 391.1 jit_solution(13737687876777263291)
XLA Ops:
  9.0 3.0 collective-permute-start.1
  14.2 16.2 %all-gather = bf16[224,1152]{1,0:T(8,128)(2,1)} all-gather(bf16[56,1152]{1,0:T(8,128)(2,1)S(1)} %fusion.30), channel_id=2, replica_groups={{0,4,8,12},{1,5,9,13},{2,6,10,14},{3,7,11,15},{16,20,24,28},{17,21,25,2..., dimensions={0}, use_global_device_ids=true | all-gather | bytes 645120 | tf_op jit(solution)/shard_map/all_gather | solution.py:268
  40.1 8.2 %collective-permute-done.4 = bf16[1,6,32,512]{3,2,1,0:T(8,128)(2,1)S(1)} collective-permute-done((bf16[1,6,32,512]{3,2,1,0:T(8,128)(2,1)S(1)}, bf16[1,6,32,512]{3,2,1,0:T(8,128)(2,1)S(1)}, u32[]{:S(2)}, u32[]{:S(2)}) %collective-permute-start.4) | collective-permute-done | bytes 196640 | tf_op jit(solution)/shard_map/ppermute | solution.py:241
  48.4 7.8 %collective-permute-done.5 = bf16[2,6,32,512]{3,2,1,0:T(8,128)(2,1)S(1)} collective-permute-done((bf16[2,6,32,512]{3,2,1,0:T(8,128)(2,1)S(1)}, bf16[2,6,32,512]{3,2,1,0:T(8,128)(2,1)S(1)}, u32[]{:S(2)}, u32[]{:S(2)}) %collective-permute-start.5) | collective-permute-done | bytes 393248 | tf_op jit(solution)/shard_map/ppermute | solution.py:241
  57.8 16.0 %collective-permute-done.6 = bf16[4,6,32,512]{3,2,1,0:T(8,128)(2,1)S(1)} collective-permute-done((bf16[4,6,32,512]{3,2,1,0:T(8,128)(2,1)S(1)}, bf16[4,6,32,512]{3,2,1,0:T(8,128)(2,1)S(1)}, u32[]{:S(2)}, u32[]{:S(2)}) %collective-permute-start.6) | collective-permute-done | bytes 786464 | tf_op jit(solution)/shard_map/ppermute | solution.py:241
  80.5 6.4 %collective-permute-done = bf16[256,768]{1,0:T(8,128)(2,1)S(1)} collective-permute-done((bf16[256,768]{1,0:T(8,128)(2,1)S(1)}, bf16[256,768]{1,0:T(8,128)(2,1)S(1)}, u32[]{:S(2)}, u32[]{:S(2)}) %collective-permute-start) | collective-permute-done | bytes 393248 | tf_op jit(solution)/shard_map/ppermute | solution.py:236
  86.8 2.9 fusion.6.q_ref.k_ref.v_ref
  92.1 3.1 collective-permute-start.2
  100.5 2.8 constant_dynamic-update-slice_fusion.table_ref
  105.1 11.8 %attend.1 = bf16[512,384]{1,0:T(8,128)(2,1)} custom-call(s32[32]{0:T(128)} %extent_ref.3, s32[17]{0:T(128)} %pad_add_fusion.info_ref, bf16[512,1152]{1,0:T(8,128)(2,1)} %copy-done, bf16[512,1152]{1,0:T(8,128)(2,1)} %copy-done, bf16[512,1152]{1,0:T(8,128)(2,1)} %copy-done, bf16[512,768]{1,0:T(8,128)(2,1)} %copy-done.2, bf16[512,768]{1,0:T(8,128)(2,1)} %copy-done.2, ...), custom_call_target="tpu_custom_call" | custom-call | tf_op jit(solution)/shard_map/attend/pallas_call | solution.py:201
  119.7 32.6 %all-gather.8.cloned.1.call-done = bf16[7168,768]{1,0:T(8,128)(2,1)} async-done(((bf16[224,768]{1,0:T(8,128)(2,1)}), bf16[7168,768]{1,0:T(8,128)(2,1)}) %all-gather.8.cloned.1.call-update) | async-done | bytes 11010064 | tf_op jit(solution)/shard_map/all_gather | solution.py:337
  153.2 4.8 %slice.268 = bf16[32,96,768]{2,1,0:T(8,128)(2,1)} slice(bf16[32,224,768]{2,1,0:T(8,128)(2,1)} %bitcast.147), slice={[0:32], [120:216], [0:768]} | slice | bytes 9437184 | tf_op jit(solution)/shard_map/slice | solution.py:388
  158.0 5.0 %fusion.50 = (bf16[32,24,768]{2,1,0:T(8,128)(2,1)S(1)}, bf16[32,24,768]{2,1,0:T(8,128)(2,1)}, bf16[32,24,768]{2,1,0:T(8,128)(2,1)}, bf16[32,24,768]{2,1,0:T(8,128)(2,1)}, bf16[32,24,768]{2,1,0:T(8,128)(2,1)}) fusion(bf16[32,224,768]{2,1,0:T(8,128)(2,1)} %bitcast.148), kind=kLoop, calls=%fused_computation.180 | loop fusion | bytes 11796480 | tf_op jit(solution)/shard_map/slice | solution.py:383
  166.4 9.3 %multiply_convert_fusion = (bf16[256,3072]{1,0:T(8,128)(2,1)S(1)}, f32[256,3072]{1,0:T(8,128)S(1)}, f32[256,3072]{1,0:T(8,128)S(1)}) fusion(f32[3072]{0:T(1024)S(1)} %add.236, bf16[768,768]{1,0:T(8,128)(2,1)S(1)} %bitcast.170, bf16[768,768]{1,0:T(8,128)(2,1)S(1)} %bitcast.172, bf16[768,768]{1,0:T(8,128)(2,1)S(1)} %bitcast.174, ...), kind=kOutput, calls=%fused_computation.10 | convolution fusion | flops 1279721472 | bytes 13389824 | tf_op jit(solution)/shard_map/dot_general | solution.py:31
  179.8 3.0 fusion.44
  184.9 3.8 convolution_convert_fusion.1
  188.7 3.6 convolution_convert_fusion
  198.2 2.7 fusion.51
  211.1 7.0 %collective-permute-done.9 = bf16[256,384]{1,0:T(8,128)(2,1)S(1)} collective-permute-done((bf16[256,384]{1,0:T(8,128)(2,1)S(1)}, bf16[256,384]{1,0:T(8,128)(2,1)S(1)}, u32[]{:S(2)}, u32[]{:S(2)}) %collective-permute-start.9) | collective-permute-done | bytes 196640 | tf_op jit(solution)/shard_map/ppermute | solution.py:236
  219.1 20.5 %attend_back.1 = (bf16[512,384]{1,0:T(8,128)(2,1)}, bf16[1536,384]{1,0:T(8,128)(2,1)}, bf16[1536,384]{1,0:T(8,128)(2,1)}, bf16[6,512,512]{2,1,0:T(8,128)(2,1)}) custom-call(s32[32]{0:T(128)} %extent_ref.3, s32[17]{0:T(128)} %pad_add_fusion.info_ref, bf16[512,1152]{1,0:T(8,128)(2,1)} %copy-done, bf16[512,1152]{1,0:T(8,128)(2,1)} %copy-done, ...), custom_call_target="tpu_custom_call" | custom-call | tf_op jit(solution)/shard_map/attend_back/pallas_call | solution.py:216
  244.1 8.4 %collective-permute-start.11 = (bf16[512,768]{1,0:T(8,128)(2,1)}, bf16[512,768]{1,0:T(8,128)(2,1)}, u32[]{:S(2)}, u32[]{:S(2)}) collective-permute-start(bf16[512,768]{1,0:T(8,128)(2,1)} %get-tuple-element.54), channel_id=1, source_target_pairs={{0,1},{1,2},{2,3},{3,4},{4,5},{5,6},{6,7},{7,8},{8,9},{9,10},{10,1... | collective-permute-start | bytes 2359304 | tf_op jit(solution)/shard_map/ppermute | solution.py:247
  257.1 2.8 convolution_convert_fusion.2
  261.9 26.9 %collective-permute-start.13 = (bf16[2,2,2,56,1152]{4,3,2,1,0:T(8,128)(2,1)}, bf16[2,2,2,56,1152]{4,3,2,1,0:T(8,128)(2,1)}, u32[]{:S(2)}, u32[]{:S(2)}) collective-permute-start(bf16[2,2,2,56,1152]{4,3,2,1,0:T(8,128)(2,1)} %fusion.10), channel_id=1, source_target_pairs={{0,1},{1,0},{2,3},{3,2},{4,5},{5,4},{6,7},{7,6},{8,9},{9,8},{10,11... | collective-permute-start | bytes 3096584 | tf_op jit(solution)/shard_map/ppermute | solution.py:241
  288.8 3.5 constant_dynamic-slice_fusion.1
  293.8 3.0 fusion.26
  298.4 2.6 collective-permute-start.14
  304.1 9.5 %collective-permute-done.14 = bf16[2,2,56,1152]{3,2,1,0:T(8,128)(2,1)S(1)} collective-permute-done((bf16[2,2,56,1152]{3,2,1,0:T(8,128)(2,1)S(1)}, bf16[2,2,56,1152]{3,2,1,0:T(8,128)(2,1)S(1)}, u32[]{:S(2)}, u32[]{:S(2)}) %collective-permute-start.14) | collective-permute-done | bytes 516128 | tf_op jit(solution)/shard_map/ppermute | solution.py:241
  315.7 16.6 %collective-permute-done.15 = bf16[2,56,1152]{2,1,0:T(8,128)(2,1)S(1)} collective-permute-done((bf16[2,56,1152]{2,1,0:T(8,128)(2,1)S(1)}, bf16[2,56,1152]{2,1,0:T(8,128)(2,1)S(1)}, u32[]{:S(2)}, u32[]{:S(2)}) %collective-permute-start.15) | collective-permute-done | bytes 258080 | tf_op jit(solution)/shard_map/ppermute | solution.py:241
  332.5 4.7 %collective-permute-done.19 = bf16[6,2,2,32,512]{4,3,0,2,1:T(8,128)(2,1)S(1)} collective-permute-done((bf16[6,2,2,32,512]{4,3,0,2,1:T(8,128)(2,1)S(1)}, bf16[6,2,2,32,512]{4,3,0,2,1:T(8,128)(2,1)S(1)}, u32[]{:S(2)}, u32[]{:S(2)}) %collective-permute-start.19) | collective-permute-done | bytes 786464 | tf_op jit(solution)/shard_map/ppermute | solution.py:241
  338.6 24.9 %collective-permute-done.20 = bf16[6,2,32,512]{3,2,0,1:T(8,128)(2,1)S(1)} collective-permute-done((bf16[6,2,32,512]{3,2,0,1:T(8,128)(2,1)S(1)}, bf16[6,2,32,512]{3,2,0,1:T(8,128)(2,1)S(1)}, u32[]{:S(2)}, u32[]{:S(2)}) %collective-permute-start.20) | collective-permute-done | bytes 393248 | tf_op jit(solution)/shard_map/ppermute | solution.py:241
  365.1 9.0 %collective-permute-done.21 = bf16[6,32,512]{2,1,0:T(8,128)(2,1)S(1)} collective-permute-done((bf16[6,32,512]{2,1,0:T(8,128)(2,1)S(1)}, bf16[6,32,512]{2,1,0:T(8,128)(2,1)S(1)}, u32[]{:S(2)}, u32[]{:S(2)}) %collective-permute-start.21) | collective-permute-done | bytes 196640 | tf_op jit(solution)/shard_map/ppermute | solution.py:241
  375.0 4.4 %reduce-scatter.2.cloned.1.call-done = bf16[1,224,768]{2,1,0:T(8,128)(2,1)} async-done(((bf16[32,224,768]{2,1,0:T(8,128)(2,1)}), bf16[1,224,768]{2,1,0:T(8,128)(2,1)}) %reduce-scatter.2.cloned.1.call-update) | async-done | bytes 344080 | tf_op jit(solution)/shard_map/reduce_scatter | solution.py:443
  (253 shorter events, 89.6 us)
Async XLA Ops:
  7.2 31.2 %copy-start.24 = (f32[6]{0:T(128)S(1)}, f32[6]{0:T(128)}, u32[]{:S(2)}) copy-start(f32[6]{0:T(128)} %param.23) | copy-start | bytes 76
  7.2 31.2 %copy-start.19 = (f32[6,32,512]{2,1,0:T(8,128)S(1)}, f32[6,32,512]{2,1,0:T(8,128)}, u32[]{:S(2)}) copy-start(f32[6,32,512]{2,1,0:T(8,128)} %param.22) | copy-start | bytes 1179652
  7.2 31.2 %copy-start.18 = (f32[6,32,512]{2,1,0:T(8,128)S(1)}, f32[6,32,512]{2,1,0:T(8,128)}, u32[]{:S(2)}) copy-start(f32[6,32,512]{2,1,0:T(8,128)} %param.21) | copy-start | bytes 1179652
  7.2 69.7 %all-gather.6.cloned.1.call-start = ((), (), s32[]{:S(2)}) async-start(), calls=%async_computation.2 | async-start | bytes 2580480 | tf_op jit(solution)/shard_map/all_gather | solution.py:269
  9.0 5.2 %collective-permute-start.1 = (bf16[24,1152]{1,0:T(8,128)(2,1)S(1)}, bf16[24,1152]{1,0:T(8,128)(2,1)S(1)}, u32[]{:S(2)}, u32[]{:S(2)}) collective-permute-start(bf16[24,1152]{1,0:T(8,128)(2,1)S(1)} %bitcast.187), channel_id=1, source_target_pairs={{0,16},{16,0},{1,17},{17,1},{2,18},{18,2},{3,19},{19,3},{4,20},{20... | collective-permute-start | bytes 165896 | tf_op jit(solution)/shard_map/ppermute | solution.py:236
  30.5 121.8 %all-gather.8.cloned.1.call-start = ((), (), s32[]{:S(2)}) async-start(), calls=%async_computation.3 | async-start | bytes 11354112 | tf_op jit(solution)/shard_map/all_gather | solution.py:337
  38.3 341.1 %reduce-scatter.2.cloned.1.call-start = ((), (), s32[]{:S(2)}) async-start(), calls=%async_computation.1 | async-start | bytes 11354112 | tf_op jit(solution)/shard_map/reduce_scatter | solution.py:443
  39.4 35.9 %copy-start.26 = (bf16[1,256,768]{2,1,0:T(8,128)(2,1)S(1)}, bf16[1,256,768]{2,1,0:T(8,128)(2,1)}, u32[]{:S(2)}) copy-start(bf16[1,256,768]{2,1,0:T(8,128)(2,1)} %param.13) | copy-start | bytes 1179652
  39.4 8.9 %collective-permute-start.4 = (bf16[1,6,32,512]{3,2,1,0:T(8,128)(2,1)S(1)}, bf16[1,6,32,512]{3,2,1,0:T(8,128)(2,1)S(1)}, u32[]{:S(2)}, u32[]{:S(2)}) collective-permute-start(bf16[1,6,32,512]{3,2,1,0:T(8,128)(2,1)S(1)} %get-tuple-element.40), channel_id=1, source_target_pairs={{0,8},{1,9},{2,10},{3,11},{4,12},{5,13},{6,14},{7,15},{8,0},{9,1},... | collective-permute-start | bytes 589832 | tf_op jit(solution)/shard_map/ppermute | solution.py:241
  48.3 7.8 %collective-permute-start.5 = (bf16[2,6,32,512]{3,2,1,0:T(8,128)(2,1)S(1)}, bf16[2,6,32,512]{3,2,1,0:T(8,128)(2,1)S(1)}, u32[]{:S(2)}, u32[]{:S(2)}) collective-permute-start(bf16[2,6,32,512]{3,2,1,0:T(8,128)(2,1)S(1)} %pad_maximum_fusion.6), channel_id=1, source_target_pairs={{0,4},{1,5},{2,6},{3,7},{4,0},{5,1},{6,2},{7,3},{8,12},{9,13},{10,... | collective-permute-start | bytes 1179656 | tf_op jit(solution)/shard_map/ppermute | solution.py:241
  56.2 17.6 %collective-permute-start.6 = (bf16[4,6,32,512]{3,2,1,0:T(8,128)(2,1)S(1)}, bf16[4,6,32,512]{3,2,1,0:T(8,128)(2,1)S(1)}, u32[]{:S(2)}, u32[]{:S(2)}) collective-permute-start(bf16[4,6,32,512]{3,2,1,0:T(8,128)(2,1)S(1)} %pad_maximum_fusion.5), channel_id=1, source_target_pairs={{0,2},{1,3},{2,0},{3,1},{4,6},{5,7},{6,4},{7,5},{8,10},{9,11},{10,... | collective-permute-start | bytes 2359304 | tf_op jit(solution)/shard_map/ppermute | solution.py:241
  75.3 25.2 %collective-permute-start.7 = (bf16[8,6,32,512]{3,2,1,0:T(8,128)(2,1)}, bf16[8,6,32,512]{3,2,1,0:T(8,128)(2,1)}, u32[]{:S(2)}, u32[]{:S(2)}) collective-permute-start(bf16[8,6,32,512]{3,2,1,0:T(8,128)(2,1)} %pad_maximum_fusion.1), channel_id=1, source_target_pairs={{0,1},{1,0},{2,3},{3,2},{4,5},{5,4},{6,7},{7,6},{8,9},{9,8},{10,11... | collective-permute-start | bytes 4718600 | tf_op jit(solution)/shard_map/ppermute | solution.py:241
  75.3 11.5 %collective-permute-start = (bf16[256,768]{1,0:T(8,128)(2,1)S(1)}, bf16[256,768]{1,0:T(8,128)(2,1)S(1)}, u32[]{:S(2)}, u32[]{:S(2)}) collective-permute-start(bf16[256,768]{1,0:T(8,128)(2,1)S(1)} %bitcast.189), channel_id=1, source_target_pairs={{0,16},{16,0},{1,17},{17,1},{2,18},{18,2},{3,19},{19,3},{4,20},{20... | collective-permute-start | bytes 1179656 | tf_op jit(solution)/shard_map/ppermute | solution.py:236
  90.8 12.5 %collective-permute-start.3 = (bf16[512,768]{1,0:T(8,128)(2,1)}, bf16[512,768]{1,0:T(8,128)(2,1)S(1)}, u32[]{:S(2)}, u32[]{:S(2)}) collective-permute-start(bf16[512,768]{1,0:T(8,128)(2,1)} %slice.256), channel_id=1, source_target_pairs={{1,0},{2,1},{3,2},{4,3},{5,4},{6,5},{7,6},{8,7},{9,8},{10,9},{11,1... | collective-permute-start | bytes 2359304 | tf_op jit(solution)/shard_map/ppermute | solution.py:247
  92.1 11.2 %collective-permute-start.2 = (bf16[512,768]{1,0:T(8,128)(2,1)}, bf16[512,768]{1,0:T(8,128)(2,1)S(1)}, u32[]{:S(2)}, u32[]{:S(2)}) collective-permute-start(bf16[512,768]{1,0:T(8,128)(2,1)} %slice.256), channel_id=1, source_target_pairs={{0,1},{1,2},{2,3},{3,4},{4,5},{5,6},{6,7},{7,8},{8,9},{9,10},{10,1... | collective-permute-start | bytes 2359304 | tf_op jit(solution)/shard_map/ppermute | solution.py:247
  117.9 46.4 %copy-start.21 = (bf16[256,384]{1,0:T(8,128)(2,1)}, bf16[256,384]{1,0:T(8,128)(2,1)S(1)}, u32[]{:S(2)}) copy-start(bf16[256,384]{1,0:T(8,128)(2,1)S(1)} %get-tuple-element.65) | copy-start | bytes 589828
  117.9 46.4 %collective-permute-start.8 = (bf16[256,384]{1,0:T(8,128)(2,1)S(1)}, bf16[256,384]{1,0:T(8,128)(2,1)S(1)}, u32[]{:S(2)}, u32[]{:S(2)}) collective-permute-start(bf16[256,384]{1,0:T(8,128)(2,1)S(1)} %get-tuple-element.66), channel_id=1, source_target_pairs={{0,16},{16,0},{1,17},{17,1},{2,18},{18,2},{3,19},{19,3},{4,20},{20... | collective-permute-start | bytes 589832 | tf_op jit(solution)/shard_map/ppermute | solution.py:236
  211.1 7.1 %collective-permute-start.9 = (bf16[256,384]{1,0:T(8,128)(2,1)S(1)}, bf16[256,384]{1,0:T(8,128)(2,1)S(1)}, u32[]{:S(2)}, u32[]{:S(2)}) collective-permute-start(bf16[256,384]{1,0:T(8,128)(2,1)S(1)} %get-tuple-element.64), channel_id=1, source_target_pairs={{0,16},{16,0},{1,17},{17,1},{2,18},{18,2},{3,19},{19,3},{4,20},{20... | collective-permute-start | bytes 589832 | tf_op jit(solution)/shard_map/ppermute | solution.py:236
  242.8 9.7 %collective-permute-start.10 = (bf16[512,768]{1,0:T(8,128)(2,1)}, bf16[512,768]{1,0:T(8,128)(2,1)}, u32[]{:S(2)}, u32[]{:S(2)}) collective-permute-start(bf16[512,768]{1,0:T(8,128)(2,1)} %get-tuple-element.53), channel_id=1, source_target_pairs={{1,0},{2,1},{3,2},{4,3},{5,4},{6,5},{7,6},{8,7},{9,8},{10,9},{11,1... | collective-permute-start | bytes 2359304 | tf_op jit(solution)/shard_map/ppermute | solution.py:247
  244.1 9.9 %collective-permute-start.11 = (bf16[512,768]{1,0:T(8,128)(2,1)}, bf16[512,768]{1,0:T(8,128)(2,1)}, u32[]{:S(2)}, u32[]{:S(2)}) collective-permute-start(bf16[512,768]{1,0:T(8,128)(2,1)} %get-tuple-element.54), channel_id=1, source_target_pairs={{0,1},{1,2},{2,3},{3,4},{4,5},{5,6},{6,7},{7,8},{8,9},{9,10},{10,1... | collective-permute-start | bytes 2359304 | tf_op jit(solution)/shard_map/ppermute | solution.py:247
  261.9 34.9 %collective-permute-start.13 = (bf16[2,2,2,56,1152]{4,3,2,1,0:T(8,128)(2,1)}, bf16[2,2,2,56,1152]{4,3,2,1,0:T(8,128)(2,1)}, u32[]{:S(2)}, u32[]{:S(2)}) collective-permute-start(bf16[2,2,2,56,1152]{4,3,2,1,0:T(8,128)(2,1)} %fusion.10), channel_id=1, source_target_pairs={{0,1},{1,0},{2,3},{3,2},{4,5},{5,4},{6,7},{7,6},{8,9},{9,8},{10,11... | collective-permute-start | bytes 3096584 | tf_op jit(solution)/shard_map/ppermute | solution.py:241
  293.6 8.2 %collective-permute-start.18 = (bf16[6,2,2,2,32,512]{5,4,0,2,1,3:T(8,128)(2,1)}, bf16[6,2,2,2,32,512]{5,4,0,2,1,3:T(8,128)(2,1)}, u32[]{:S(2)}, u32[]{:S(2)}) collective-permute-start(bf16[6,2,2,2,32,512]{5,4,0,2,1,3:T(8,128)(2,1)} %bitcast.138), channel_id=1, source_target_pairs={{0,1},{1,0},{2,3},{3,2},{4,5},{5,4},{6,7},{7,6},{8,9},{9,8},{10,11... | collective-permute-start | bytes 4718600 | tf_op jit(solution)/shard_map/ppermute | solution.py:241
  298.4 15.2 %collective-permute-start.14 = (bf16[2,2,56,1152]{3,2,1,0:T(8,128)(2,1)S(1)}, bf16[2,2,56,1152]{3,2,1,0:T(8,128)(2,1)S(1)}, u32[]{:S(2)}, u32[]{:S(2)}) collective-permute-start(bf16[2,2,56,1152]{3,2,1,0:T(8,128)(2,1)S(1)} %fusion.19), channel_id=1, source_target_pairs={{0,2},{1,3},{2,0},{3,1},{4,6},{5,7},{6,4},{7,5},{8,10},{9,11},{10,... | collective-permute-start | bytes 1548296 | tf_op jit(solution)/shard_map/ppermute | solution.py:241
  301.1 13.5 %collective-permute-start.12 = (bf16[256,768]{1,0:T(8,128)(2,1)S(1)}, bf16[256,768]{1,0:T(8,128)(2,1)S(1)}, u32[]{:S(2)}, u32[]{:S(2)}) collective-permute-start(bf16[256,768]{1,0:T(8,128)(2,1)S(1)} %dynamic-slice_convert_fusion.3), channel_id=1, source_target_pairs={{0,16},{16,0},{1,17},{17,1},{2,18},{18,2},{3,19},{19,3},{4,20},{20... | collective-permute-start | bytes 1179656 | tf_op jit(solution)/shard_map/ppermute | solution.py:236
  304.1 33.1 %collective-permute-start.19 = (bf16[6,2,2,32,512]{4,3,0,2,1:T(8,128)(2,1)S(1)}, bf16[6,2,2,32,512]{4,3,0,2,1:T(8,128)(2,1)S(1)}, u32[]{:S(2)}, u32[]{:S(2)}) collective-permute-start(bf16[6,2,2,32,512]{4,3,0,2,1:T(8,128)(2,1)S(1)} %fusion.17), channel_id=1, source_target_pairs={{0,2},{1,3},{2,0},{3,1},{4,6},{5,7},{6,4},{7,5},{8,10},{9,11},{10,... | collective-permute-start | bytes 2359304 | tf_op jit(solution)/shard_map/ppermute | solution.py:241
  313.8 18.5 %collective-permute-start.15 = (bf16[2,56,1152]{2,1,0:T(8,128)(2,1)S(1)}, bf16[2,56,1152]{2,1,0:T(8,128)(2,1)S(1)}, u32[]{:S(2)}, u32[]{:S(2)}) collective-permute-start(bf16[2,56,1152]{2,1,0:T(8,128)(2,1)S(1)} %fusion.27), channel_id=1, source_target_pairs={{0,8},{1,9},{2,10},{3,11},{4,12},{5,13},{6,14},{7,15},{8,0},{9,1},... | collective-permute-start | bytes 774152 | tf_op jit(solution)/shard_map/ppermute | solution.py:241
  332.4 5.7 %collective-permute-start.16 = (bf16[56,1152]{1,0:T(8,128)(2,1)S(1)}, bf16[56,1152]{1,0:T(8,128)(2,1)S(1)}, u32[]{:S(2)}, u32[]{:S(2)}) collective-permute-start(bf16[56,1152]{1,0:T(8,128)(2,1)S(1)} %fusion.31), channel_id=1, source_target_pairs={{0,4},{1,5},{2,6},{3,7},{4,0},{5,1},{6,2},{7,3},{8,12},{9,13},{10,... | collective-permute-start | bytes 387080 | tf_op jit(solution)/shard_map/ppermute | solution.py:241
  337.4 36.7 %copy-start.11 = (f32[6,32,512]{2,1,0:T(8,128)S(1)}, f32[6,32,512]{2,1,0:T(8,128)}, u32[]{:S(2)}) copy-start(f32[6,32,512]{2,1,0:T(8,128)} %get-tuple-element.41) | copy-start | bytes 1179652
  337.4 36.7 %copy-start.25 = (f32[6]{0:T(128)S(1)}, f32[6]{0:T(128)}, u32[]{:S(2)}) copy-start(f32[6]{0:T(128)} %param.23) | copy-start | bytes 76
  337.5 26.0 %collective-permute-start.20 = (bf16[6,2,32,512]{3,2,0,1:T(8,128)(2,1)S(1)}, bf16[6,2,32,512]{3,2,0,1:T(8,128)(2,1)S(1)}, u32[]{:S(2)}, u32[]{:S(2)}) collective-permute-start(bf16[6,2,32,512]{3,2,0,1:T(8,128)(2,1)S(1)} %fusion.21), channel_id=1, source_target_pairs={{0,8},{1,9},{2,10},{3,11},{4,12},{5,13},{6,14},{7,15},{8,0},{9,1},... | collective-permute-start | bytes 1179656 | tf_op jit(solution)/shard_map/ppermute | solution.py:241
  338.1 25.8 %collective-permute-start.17 = (bf16[24,1152]{1,0:T(8,128)(2,1)S(1)}, bf16[24,1152]{1,0:T(8,128)(2,1)S(1)}, u32[]{:S(2)}, u32[]{:S(2)}) collective-permute-start(bf16[24,1152]{1,0:T(8,128)(2,1)S(1)} %fusion.32), channel_id=1, source_target_pairs={{0,16},{16,0},{1,17},{17,1},{2,18},{18,2},{3,19},{19,3},{4,20},{20... | collective-permute-start | bytes 165896 | tf_op jit(solution)/shard_map/ppermute | solution.py:236
  363.7 10.4 %collective-permute-start.21 = (bf16[6,32,512]{2,1,0:T(8,128)(2,1)S(1)}, bf16[6,32,512]{2,1,0:T(8,128)(2,1)S(1)}, u32[]{:S(2)}, u32[]{:S(2)}) collective-permute-start(bf16[6,32,512]{2,1,0:T(8,128)(2,1)S(1)} %fusion.29), channel_id=1, source_target_pairs={{0,4},{1,5},{2,6},{3,7},{4,0},{5,1},{6,2},{7,3},{8,12},{9,13},{10,... | collective-permute-start | bytes 589832 | tf_op jit(solution)/shard_map/ppermute | solution.py:241
  (28 other events, 164.6 us)
Sparse Core Ops, SparseCore 0:
  30.6 24.1 all-gather.5
  57.7 94.5 all-gather.7
  210.6 168.7 reduce-scatter.1
